TPU v7x, 512 devices: a whole 4x4x16 slice. The times are simulated.
512 devices in a mesh: en: 32 (over z, x_hi), ph: 4 (over y), blk: 4 (over x_lo, core).
Axes of the slice: x: 4 (x_hi: 2, x_lo: 2; x = x_hi * 2 + x_lo), y: 4, z: 16, core: 2. Of those that a mesh axis runs over, the one named last changes fastest.
Arguments:
- lesser_in: bfloat16 [96, 8, 512, 512], P('en', 'blk', 'ph'), may hold values from -6 to 6
- greater_in: bfloat16 [96, 8, 512, 512], P('en', 'blk', 'ph'), may hold values from -6 to 6
- inverse: bfloat16 [96, 8, 512, 512], P('en', 'blk', 'ph'), may hold values from -0.25 to 0.25
- offsets: int32 [96, 8], P('en', 'ph'), may hold values from -9 to 9, as said below
- couplings: float32 [96, 8], P('en', 'ph'), may hold values from 0.2 to 1
Outputs:
- lesser_out: bfloat16 [96, 8, 512, 512], P('en', 'blk', 'ph')
- greater_out: bfloat16 [96, 8, 512, 512], P('en', 'blk', 'ph')
Inputs may be any that keep to these rules, and one draw needn't show every extreme that they name: `offsets`: both extremes occur in every draw.
All inputs are finite; a program needn't handle non-finite values.
Results may differ from a plain program's by a relative error of at most 0.0057.
Values may be sent and summed in bfloat16 or wider, within the bound.
A program may use at most 64 MiB of HBM per device.

v0:
```python
import functools

import jax
import jax.numpy as jnp
from jax import lax
from jax.experimental import pallas as pl
from jax.experimental.pallas import tpu as pltpu
from jax.sharding import PartitionSpec as P

MESH = pl.DeviceIdType.MESH
MAXOFF = 9
CHUNKS = 4
EXTRA = 3
ROWS = 64


def owner(chunk, j):
    if j == 2:
        return (chunk + 2) % 4
    return 2 * j + 1 - chunk % 2


def kernel(
    n_en, offs_ref, coup_ref, less_ref, great_ref, inv_ref,
    less_out, great_out,
    win0, win1, win2, win3, sig, whole, invs, prod, offs_v, coup_v, offs_s, coup_s,
    win_recv, x_send, z_send, sig_send, sig_recv, inv_send, inv_recv,
    out_send, out_recv, meta_send, meta_recv, smem_sem,
):
    wins = (win0, win1, win2, win3)
    en, y = lax.axis_index("en"), lax.axis_index("ph")
    h = lax.rem(en, 2)
    base = en - h
    up = {"en": lax.rem(en + 2, n_en)}
    down = {"en": lax.rem(en + n_en - 2, n_en)}
    partner = {"en": base + 1 - h}

    def group_member(d):
        return {"en": base + lax.rem(h + d // 4, 2), "ph": lax.rem(y + d % 4, 4)}

    barrier = pltpu.get_barrier_semaphore()
    pl.semaphore_signal(barrier, inc=1, device_id=up, device_id_type=MESH)
    pl.semaphore_signal(barrier, inc=1, device_id=down, device_id_type=MESH)
    for d in range(1, 8):
        pl.semaphore_signal(barrier, inc=1, device_id=group_member(d), device_id_type=MESH)
    pl.semaphore_wait(barrier, 9)

    def remote(src, dst, send, recv, device):
        return pltpu.make_async_remote_copy(
            src_ref=src, dst_ref=dst, send_sem=send, recv_sem=recv, device_id=device, device_id_type=MESH
        )

    def source(chunk, half):
        ref = (less_ref, great_ref)[chunk // 2]
        return ref.at[:, chunk % 2, pl.ds(pl.multiple_of(half * ROWS, ROWS), ROWS), :]

    def group(chunk, g):
        return wins[chunk].at[pl.ds(3 * g, 3)]

    def wait_group(chunk, g):
        pltpu.make_async_copy(group(chunk, g), group(chunk, g), win_recv.at[chunk, g]).wait()

    def own_local(chunk):
        return pltpu.make_async_copy(source(chunk, h), group(chunk, 3 + h), win_recv.at[chunk, 3 + h])

    def exchange(chunk):
        return remote(source(chunk, 1 - h), group(chunk, 3 + h), x_send.at[chunk], win_recv.at[chunk, 3 + h], partner)

    def own(chunk):
        src = source(chunk, h)
        return (
            remote(src, group(chunk, 1 + h), z_send.at[chunk, 0], win_recv.at[chunk, 1 + h], up),
            remote(src, group(chunk, 5 + h), z_send.at[chunk, 1], win_recv.at[chunk, 5 + h], down),
        )

    def passed(chunk):
        src = group(chunk, 4 - h)
        return (
            remote(src, group(chunk, 2 - h), z_send.at[chunk, 2], win_recv.at[chunk, 2 - h], up),
            remote(src, group(chunk, 6 - h), z_send.at[chunk, 3], win_recv.at[chunk, 6 - h], down),
        )

    def relay(chunk):
        return (
            remote(group(chunk, 2), group(chunk, 0), z_send.at[chunk, 4], win_recv.at[chunk, 0], up),
            remote(group(chunk, 5), group(chunk, 7), z_send.at[chunk, 5], win_recv.at[chunk, 7], down),
        )

    def start(copies):
        for copy in copies:
            copy.start()

    def inv_part(slot, to):
        if slot == 0:
            return inv_ref.at[to // 2, 1 - lax.rem(to, 2)]
        return inv_ref.at[2, lax.rem(to, 2)]

    def inv_copy(slot, d):
        to = lax.rem(y + d, 4)
        return remote(inv_part(slot, to), invs.at[slot, y], inv_send.at[slot, d - 1], inv_recv.at[slot, y], {"ph": to})

    def meta_copies(d):
        me = 4 * h + y
        to = group_member(d)
        return (
            remote(offs_ref, offs_v.at[me], meta_send.at[0, d], meta_recv.at[0, me], to),
            remote(coup_ref, coup_v.at[me], meta_send.at[1, d], meta_recv.at[1, me], to),
        )

    exchange(0).start()
    start(own(0))
    me = 4 * h + y
    pltpu.make_async_copy(offs_ref, offs_v.at[me], meta_recv.at[0, me]).start()
    pltpu.make_async_copy(coup_ref, coup_v.at[me], meta_recv.at[1, me]).start()
    for d in range(1, 8):
        start(meta_copies(d))
    start(own(1))
    for chunk in range(1, CHUNKS):
        exchange(chunk).start()
    for slot in range(2):
        pltpu.make_async_copy(inv_part(slot, y), invs.at[slot, y], inv_recv.at[slot, y]).start()
        for d in range(1, 4):
            inv_copy(slot, d).start()
    for chunk in range(CHUNKS):
        own_local(chunk).start()

    def forward(chunk):
        wait_group(chunk, 4 - h)
        start(passed(chunk))

    def relays(chunk):
        wait_group(chunk, 2)
        wait_group(chunk, 5)
        start(relay(chunk))

    def gather_meta():
        for m in range(8):
            pltpu.make_async_copy(offs_v.at[m], offs_v.at[m], meta_recv.at[0, m]).wait()
            pltpu.make_async_copy(coup_v.at[m], coup_v.at[m], meta_recv.at[1, m]).wait()
        first = pltpu.make_async_copy(offs_v, offs_s, smem_sem.at[0])
        second = pltpu.make_async_copy(coup_v, coup_s, smem_sem.at[1])
        first.start()
        second.start()
        first.wait()
        second.wait()

    def sigma_copy(chunk, n):
        to = {"en": base + n // 3, "ph": owner(chunk, n % 3)}
        part = 2 * y + h
        return remote(
            sig.at[chunk, n], whole.at[chunk, part], sig_send.at[chunk, n], sig_recv.at[chunk, part], to
        )

    def is_own(chunk, n):
        return jnp.logical_and(h == n // 3, y == owner(chunk, n % 3))

    def mix(chunk):
        for g in (0, 1, 6, 7):
            wait_group(chunk, g)
        wait_group(chunk, 3 + h)
        window = wins[chunk]

        def body(step, _):
            i = step // 2
            rows = pl.ds(pl.multiple_of(32 * lax.rem(step, 2), 32), 32)
            total = jnp.zeros((32, window.shape[2]), jnp.float32)
            for k in range(8):
                m = 4 * (i // 3) + k // 2
                offset = offs_s[m, lax.rem(i, 3), k % 2]
                energy = 3 * base + i + offset
                inside = jnp.logical_and(energy >= 0, energy < 3 * n_en)
                weight = jnp.where(inside, coup_s[m, lax.rem(i, 3), k % 2], jnp.float32(0.0))
                total = total + weight * window[i + offset + MAXOFF, rows, :].astype(jnp.float32)
            sig[chunk, i, rows, :] = total.astype(jnp.bfloat16)
            return 0

        lax.fori_loop(0, 12, body, 0)
        part = 2 * y + h
        for n in range(6):
            mine = is_own(chunk, n)

            @pl.when(mine)
            def _():
                pltpu.make_async_copy(sig.at[chunk, n], whole.at[chunk, part], sig_recv.at[chunk, part]).start()

            @pl.when(jnp.logical_not(mine))
            def _():
                sigma_copy(chunk, n).start()

    def out_ref(chunk, j):
        return (less_out, great_out)[chunk // 2].at[j, chunk % 2]

    def energy_of(chunk):
        return jnp.where(y == (chunk + 2) % 4, 2, y // 2)

    def out_copy(chunk, d):
        to = lax.rem(y + d, 4)
        j = energy_of(chunk)
        return remote(prod.at[chunk, to], out_ref(chunk, j), out_send.at[chunk, d], out_recv.at[chunk, j], {"ph": to})

    def multiply(chunk):
        @pl.when(y != chunk)
        def _():
            slot = jnp.where(y == (chunk + 2) % 4, 1, 0)
            for part in range(8):
                pltpu.make_async_copy(
                    whole.at[chunk, part], whole.at[chunk, part], sig_recv.at[chunk, part]
                ).wait()
            sigma = whole[chunk].reshape(512, 512)
            inverse = invs[slot].reshape(512, 512)

            for r in range(2):
                rows = invs[slot, pl.ds(2 * r, 2)].reshape(256, 512)
                left = jnp.dot(rows, sigma, preferred_element_type=jnp.float32).astype(jnp.bfloat16)
                result = lax.dot_general(
                    left, inverse, (((1,), (1,)), ((), ())), preferred_element_type=jnp.float32
                )
                prod[chunk, pl.ds(2 * r, 2)] = result.astype(jnp.bfloat16).reshape(2, 128, 512)
            for d in (2, 1, 3):
                out_copy(chunk, d).start()
            j = energy_of(chunk)
            pltpu.make_async_copy(prod.at[chunk, y], out_ref(chunk, j), out_recv.at[chunk, j]).start()

    forward(0)
    start(own(2))
    gather_meta()
    relays(0)
    forward(1)
    start(own(3))
    mix(0)
    relays(1)
    forward(2)
    for slot in range(2):
        for part in range(4):
            pltpu.make_async_copy(invs.at[slot, part], invs.at[slot, part], inv_recv.at[slot, part]).wait()
    multiply(0)
    mix(1)
    relays(2)
    forward(3)
    multiply(1)
    mix(2)
    relays(3)
    multiply(2)
    mix(3)
    multiply(3)

    for chunk in range(CHUNKS):
        exchange(chunk).wait_send()
        for copy in own(chunk) + passed(chunk) + relay(chunk):
            copy.wait_send()
        for n in range(6):

            @pl.when(jnp.logical_not(is_own(chunk, n)))
            def _():
                sigma_copy(chunk, n).wait_send()

        @pl.when(y != chunk)
        def _():
            for d in range(1, 4):
                out_copy(chunk, d).wait_send()

    for slot in range(2):
        for d in range(1, 4):
            inv_copy(slot, d).wait_send()
    for d in range(1, 8):
        for copy in meta_copies(d):
            copy.wait_send()
    for chunk in range(CHUNKS):
        for j in range(3):
            pltpu.make_async_copy(out_ref(chunk, j), out_ref(chunk, j), out_recv.at[chunk, j]).wait()


def on_device(n_en, lesser_in, greater_in, inverse, offsets, couplings):
    bf16 = jnp.bfloat16
    dma = pltpu.SemaphoreType.DMA
    any_space = pl.BlockSpec(memory_space=pl.ANY)
    vmem = pl.BlockSpec(memory_space=pltpu.VMEM)
    width = lesser_in.shape[-1]
    window = pltpu.VMEM((24, ROWS, width), bf16)
    return pl.pallas_call(
        functools.partial(kernel, n_en),
        out_shape=(
            jax.ShapeDtypeStruct(lesser_in.shape, bf16),
            jax.ShapeDtypeStruct(greater_in.shape, bf16),
        ),
        in_specs=[vmem, vmem, any_space, any_space, any_space],
        out_specs=(any_space, any_space),
        scratch_shapes=[
            window, window, window, window,
            pltpu.VMEM((CHUNKS, 6, ROWS, width), bf16),
            pltpu.VMEM((CHUNKS, 8, ROWS, width), bf16),
            pltpu.VMEM((2, 4, 128, width), bf16),
            pltpu.VMEM((CHUNKS, 4, 128, width), bf16),
            pltpu.VMEM((8, 3, 2), jnp.int32),
            pltpu.VMEM((8, 3, 2), jnp.float32),
            pltpu.SMEM((8, 3, 2), jnp.int32),
            pltpu.SMEM((8, 3, 2), jnp.float32),
            dma((CHUNKS, 8)),
            dma((CHUNKS,)),
            dma((CHUNKS, 6)),
            dma((CHUNKS, 6)),
            dma((CHUNKS, 8)),
            dma((2, 3)),
            dma((2, 4)),
            dma((CHUNKS, 4)),
            dma((CHUNKS, 3)),
            dma((2, 8)),
            dma((2, 8)),
            dma((2,)),
        ],
        compiler_params=pltpu.CompilerParams(collective_id=0, has_side_effects=True),
        name="born_update",
    )(offsets, couplings, lesser_in, greater_in, inverse)


def solution(mesh):
    blocks = P("en", "blk", "ph", None)
    placed = (blocks, blocks, blocks, P("en", "ph"), P("en", "ph"))
    return jax.shard_map(
        functools.partial(on_device, mesh.shape["en"]),
        mesh=mesh,
        in_specs=placed,
        out_specs=(blocks, blocks),
        check_vma=False,
    )
```

profile of v0, /device:TPU:6, one launch (start us, length us, event | category | flops | bytes accessed | tf_op | source)
XLA Modules:
  0.0 101.1 jit_solution(959217604597133129)
XLA Ops:
  0.6 0.0 copy-start.1
  0.6 1.3 %copy.7.offs_ref = s32[3,2]{1,0:T(4,128)} copy(s32[3,2]{0,1:T(2,128)} %param.8) | data formatting | bytes 48 | tf_op args[3]
  2.0 0.0 copy-done.1
  2.0 0.7 copy.8.coup_ref
  2.6 95.4 %born_update.1 = (bf16[3,2,128,512]{3,2,1,0:T(8,128)(2,1)}, bf16[3,2,128,512]{3,2,1,0:T(8,128)(2,1)}) custom-call(s32[3,2]{1,0:T(4,128)} %copy.7.offs_ref, f32[3,2]{1,0:T(4,128)} %copy.8.coup_ref, bf16[3,2,128,512]{3,2,1,0:T(8,128)(2,1)} %less_ref.1, bf16[3,2,128,512]{3,2,1,0:T(8,128)(2,1)} %great_ref.1, bf16[3,2,128,512]{3,2,1,0:T(8,128)(2,1)} %inv_ref.1), custom_call_target="tpu_custom_call" | custom-call | tf_op jit(solution)/shard_map/born_update/pallas_call | solution.py:280
  98.0 0.0 copy-start
  98.1 2.2 %copy.11 = bf16[3,2,128,512]{3,2,1,0:T(8,128)(2,1)} copy(bf16[3,2,128,512]{3,2,1,0:T(8,128)(2,1)} %get-tuple-element.4) | data formatting | bytes 1572864
  100.2 0.0 copy-done
  100.2 0.9 copy.12
Async XLA Ops:
  0.6 1.4 %copy-start.1 = (f32[3,2]{0,1:T(2,128)S(1)}, f32[3,2]{0,1:T(2,128)}, u32[]{:S(2)}) copy-start(f32[3,2]{0,1:T(2,128)} %param.9) | copy-start | bytes 76
  98.0 2.2 %copy-start = (bf16[3,2,128,512]{3,2,1,0:T(8,128)(2,1)S(1)}, bf16[3,2,128,512]{3,2,1,0:T(8,128)(2,1)}, u32[]{:S(2)}) copy-start(bf16[3,2,128,512]{3,2,1,0:T(8,128)(2,1)} %get-tuple-element.5) | copy-start | bytes 2359300
where the time goes:
time: 101 us
  Pallas kernels  95.4 us (94%)
  local copies, waits for them, and re-layouts  5.06 us (5%)
    pallas_call x1, Pallas kernels, on_device(): pl.pallas_call(functools.partial(kernel, n_en), out_shape=(jax.ShapeDtype...  95.4 us
    unnamed x8, local copies, waits for them, and re-layouts  5.06 us

commit v1 on v0

--- a/solution.py
+++ b/solution.py
@@ -31,6 +31,8 @@
     en, y = lax.axis_index("en"), lax.axis_index("ph")
     h = lax.rem(en, 2)
     base = en - h
+    above, below = en + 2 < n_en, en >= 2
+    two_above, two_below = en + 4 < n_en, en >= 4
     up = {"en": lax.rem(en + 2, n_en)}
     down = {"en": lax.rem(en + n_en - 2, n_en)}
     partner = {"en": base + 1 - h}
@@ -39,17 +41,23 @@
         return {"en": base + lax.rem(h + d // 4, 2), "ph": lax.rem(y + d % 4, 4)}
 
     barrier = pltpu.get_barrier_semaphore()
-    pl.semaphore_signal(barrier, inc=1, device_id=up, device_id_type=MESH)
-    pl.semaphore_signal(barrier, inc=1, device_id=down, device_id_type=MESH)
+    for side, there in ((up, above), (down, below)):
+
+        @pl.when(there)
+        def _():
+            pl.semaphore_signal(barrier, inc=1, device_id=side, device_id_type=MESH)
+
     for d in range(1, 8):
         pl.semaphore_signal(barrier, inc=1, device_id=group_member(d), device_id_type=MESH)
-    pl.semaphore_wait(barrier, 9)
+    pl.semaphore_wait(barrier, 7 + above.astype(jnp.int32) + below.astype(jnp.int32))
 
     def remote(src, dst, send, recv, device):
         return pltpu.make_async_remote_copy(
             src_ref=src, dst_ref=dst, send_sem=send, recv_sem=recv, device_id=device, device_id_type=MESH
         )
 
+    passes = (jnp.logical_and(above, below),) * 2
+
     def source(chunk, half):
         ref = (less_ref, great_ref)[chunk // 2]
         return ref.at[:, chunk % 2, pl.ds(pl.multiple_of(half * ROWS, ROWS), ROWS), :]
@@ -80,15 +88,37 @@
             remote(src, group(chunk, 6 - h), z_send.at[chunk, 3], win_recv.at[chunk, 6 - h], down),
         )
 
+    def planes(chunk):
+        return (
+            remote(group(chunk, 4), group(chunk, 2), z_send.at[chunk, 0], win_recv.at[chunk, 2], up),
+            remote(group(chunk, 3), group(chunk, 5), z_send.at[chunk, 1], win_recv.at[chunk, 5], down),
+            remote(group(chunk, 3), group(chunk, 1), z_send.at[chunk, 2], win_recv.at[chunk, 1], up),
+            remote(group(chunk, 4), group(chunk, 6), z_send.at[chunk, 3], win_recv.at[chunk, 6], down),
+        )
+
     def relay(chunk):
         return (
             remote(group(chunk, 2), group(chunk, 0), z_send.at[chunk, 4], win_recv.at[chunk, 0], up),
             remote(group(chunk, 5), group(chunk, 7), z_send.at[chunk, 5], win_recv.at[chunk, 7], down),
         )
 
-    def start(copies):
-        for copy in copies:
-            copy.start()
+    def each(copies, act, conditions):
+        for copy, there in zip(copies, conditions):
+
+            @pl.when(there)
+            def _():
+                act(copy)
+
+    def start(copies, conditions=None):
+        each(copies, lambda copy: copy.start(), conditions or (above, below))
+
+    def wait_groups(chunk, groups):
+        there = (two_below, below, below, True, True, above, above, two_above)
+        for g in groups:
+            if there[g] is True:
+                wait_group(chunk, g)
+            else:
+                pl.when(there[g])(functools.partial(wait_group, chunk, g))
 
     def inv_part(slot, to):
         if slot == 0:
@@ -113,7 +143,8 @@
     pltpu.make_async_copy(offs_ref, offs_v.at[me], meta_recv.at[0, me]).start()
     pltpu.make_async_copy(coup_ref, coup_v.at[me], meta_recv.at[1, me]).start()
     for d in range(1, 8):
-        start(meta_copies(d))
+        for copy in meta_copies(d):
+            copy.start()
     start(own(1))
     for chunk in range(1, CHUNKS):
         exchange(chunk).start()
@@ -125,13 +156,17 @@
         own_local(chunk).start()
 
     def forward(chunk):
-        wait_group(chunk, 4 - h)
-        start(passed(chunk))
+        if chunk < 2:
+            wait_group(chunk, 4 - h)
+            start(passed(chunk))
+        else:
+            wait_group(chunk, 3)
+            wait_group(chunk, 4)
+            start(planes(chunk), (above, below, above, below))
 
     def relays(chunk):
-        wait_group(chunk, 2)
-        wait_group(chunk, 5)
-        start(relay(chunk))
+        wait_groups(chunk, (2, 5))
+        start(relay(chunk), passes)
 
     def gather_meta():
         for m in range(8):
@@ -155,9 +190,9 @@
         return jnp.logical_and(h == n // 3, y == owner(chunk, n % 3))
 
     def mix(chunk):
-        for g in (0, 1, 6, 7):
-            wait_group(chunk, g)
-        wait_group(chunk, 3 + h)
+        wait_groups(chunk, (1, 6, 0, 7))
+        if chunk < 2:
+            wait_group(chunk, 3 + h)
         window = wins[chunk]
 
         def body(step, _):
@@ -166,11 +201,12 @@
             total = jnp.zeros((32, window.shape[2]), jnp.float32)
             for k in range(8):
                 m = 4 * (i // 3) + k // 2
-                offset = offs_s[m, lax.rem(i, 3), k % 2]
+                offset = offs_s[m, k % 2, lax.rem(i, 3)]
                 energy = 3 * base + i + offset
                 inside = jnp.logical_and(energy >= 0, energy < 3 * n_en)
-                weight = jnp.where(inside, coup_s[m, lax.rem(i, 3), k % 2], jnp.float32(0.0))
-                total = total + weight * window[i + offset + MAXOFF, rows, :].astype(jnp.float32)
+                weight = jnp.where(inside, coup_s[m, k % 2, lax.rem(i, 3)], jnp.float32(0.0))
+                slot = jnp.where(inside, i + offset + MAXOFF, MAXOFF)
+                total = total + weight * window[slot, rows, :].astype(jnp.float32)
             sig[chunk, i, rows, :] = total.astype(jnp.bfloat16)
             return 0
 
@@ -221,24 +257,25 @@
             j = energy_of(chunk)
             pltpu.make_async_copy(prod.at[chunk, y], out_ref(chunk, j), out_recv.at[chunk, j]).start()
 
+    def gather_inverses():
+        for slot in range(2):
+            for part in range(4):
+                pltpu.make_async_copy(invs.at[slot, part], invs.at[slot, part], inv_recv.at[slot, part]).wait()
+
     forward(0)
-    start(own(2))
     gather_meta()
+    forward(1)
     relays(0)
-    forward(1)
-    start(own(3))
-    mix(0)
     relays(1)
     forward(2)
-    for slot in range(2):
-        for part in range(4):
-            pltpu.make_async_copy(invs.at[slot, part], invs.at[slot, part], inv_recv.at[slot, part]).wait()
-    multiply(0)
+    mix(0)
     mix(1)
     relays(2)
     forward(3)
+    gather_inverses()
+    multiply(0)
+    mix(2)
     multiply(1)
-    mix(2)
     relays(3)
     multiply(2)
     mix(3)
@@ -246,8 +283,8 @@
 
     for chunk in range(CHUNKS):
         exchange(chunk).wait_send()
-        for copy in own(chunk) + passed(chunk) + relay(chunk):
-            copy.wait_send()
+        sent = (own(chunk) + passed(chunk) if chunk < 2 else planes(chunk)) + relay(chunk)
+        each(sent, lambda copy: copy.wait_send(), (above, below, above, below) + passes)
         for n in range(6):
 
             @pl.when(jnp.logical_not(is_own(chunk, n)))
@@ -291,10 +328,10 @@
             pltpu.VMEM((CHUNKS, 8, ROWS, width), bf16),
             pltpu.VMEM((2, 4, 128, width), bf16),
             pltpu.VMEM((CHUNKS, 4, 128, width), bf16),
-            pltpu.VMEM((8, 3, 2), jnp.int32),
-            pltpu.VMEM((8, 3, 2), jnp.float32),
-            pltpu.SMEM((8, 3, 2), jnp.int32),
-            pltpu.SMEM((8, 3, 2), jnp.float32),
+            pltpu.VMEM((8, 2, 3), jnp.int32),
+            pltpu.VMEM((8, 2, 3), jnp.float32),
+            pltpu.SMEM((8, 2, 3), jnp.int32),
+            pltpu.SMEM((8, 2, 3), jnp.float32),
             dma((CHUNKS, 8)),
             dma((CHUNKS,)),
             dma((CHUNKS, 6)),
@@ -308,9 +345,9 @@
             dma((2, 8)),
             dma((2,)),
         ],
-        compiler_params=pltpu.CompilerParams(collective_id=0, has_side_effects=True),
+        compiler_params=pltpu.CompilerParams(collective_id=0, has_side_effects=True, vmem_limit_bytes=40 * 1024 * 1024),
         name="born_update",
-    )(offsets, couplings, lesser_in, greater_in, inverse)
+    )(offsets.T, couplings.T, *(pltpu.with_memory_space_constraint(a, pltpu.HBM) for a in (lesser_in, greater_in, inverse)))
 
 
 def solution(mesh):

time: 101 us -> 83.3 us (0.82)
  the two profiles are of different devices: /device:TPU:6 before, /device:TPU:100 now
where the time goes in v1:
time: 83.3 us; the launch traced here: 83.2 us
  Pallas kernels  80.1 us (96%)
  local copies, waits for them, and re-layouts  2.44 us (3%)
    pallas_call x1, Pallas kernels, on_device(): pl.pallas_call(functools.partial(kernel, n_en), out_shape=(jax.ShapeDtype...  80.1 us
    unnamed x6, local copies, waits for them, and re-layouts  2.44 us

profile of v1, /device:TPU:100, one launch (start us, length us, event | category | flops | bytes accessed | tf_op | source)
XLA Modules:
  0.0 83.2 jit_solution(2714161802743058511)
XLA Ops:
  0.6 0.0 copy-start.1
  0.6 0.0 copy-start
  0.7 0.7 copy-done.1
  1.3 0.0 copy-done
  1.3 80.1 %born_update.1 = (bf16[3,2,128,512]{3,2,1,0:T(8,128)(2,1)S(1)}, bf16[3,2,128,512]{3,2,1,0:T(8,128)(2,1)S(1)}) custom-call(s32[2,3]{1,0:T(2,128)S(1)} %bitcast.2, f32[2,3]{1,0:T(2,128)S(1)} %bitcast.3, bf16[3,2,128,512]{3,2,1,0:T(8,128)(2,1)} %less_ref.1, bf16[3,2,128,512]{3,2,1,0:T(8,128)(2,1)} %great_ref.1, bf16[3,2,128,512]{3,2,1,0:T(8,128)(2,1)} %inv_ref.1), custom_call_target="tpu_custom_call" | custom-call | tf_op jit(solution)/shard_map/born_update/pallas_call | solution.py:317
  81.5 0.9 %copy.9 = bf16[3,2,128,512]{3,2,1,0:T(8,128)(2,1)} copy(bf16[3,2,128,512]{3,2,1,0:T(8,128)(2,1)S(1)} %get-tuple-element.4) | data formatting | bytes 1572864
  82.3 0.9 %copy.10 = bf16[3,2,128,512]{3,2,1,0:T(8,128)(2,1)} copy(bf16[3,2,128,512]{3,2,1,0:T(8,128)(2,1)S(1)} %get-tuple-element.5) | data formatting | bytes 1572864
Async XLA Ops:
  0.6 0.7 copy-start.1
  0.6 0.7 copy-start

commit v2 on v1

--- a/solution.py
+++ b/solution.py
@@ -195,24 +195,23 @@
             wait_group(chunk, 3 + h)
         window = wins[chunk]
 
-        def body(step, _):
-            i = step // 2
-            rows = pl.ds(pl.multiple_of(32 * lax.rem(step, 2), 32), 32)
+        def body(i, step, _):
+            rows = pl.ds(pl.multiple_of(32 * step, 32), 32)
             total = jnp.zeros((32, window.shape[2]), jnp.float32)
             for k in range(8):
                 m = 4 * (i // 3) + k // 2
-                offset = offs_s[m, k % 2, lax.rem(i, 3)]
+                offset = offs_s[m, k % 2, i % 3]
                 energy = 3 * base + i + offset
                 inside = jnp.logical_and(energy >= 0, energy < 3 * n_en)
-                weight = jnp.where(inside, coup_s[m, k % 2, lax.rem(i, 3)], jnp.float32(0.0))
+                weight = jnp.where(inside, coup_s[m, k % 2, i % 3], jnp.float32(0.0))
                 slot = jnp.where(inside, i + offset + MAXOFF, MAXOFF)
                 total = total + weight * window[slot, rows, :].astype(jnp.float32)
             sig[chunk, i, rows, :] = total.astype(jnp.bfloat16)
             return 0
 
-        lax.fori_loop(0, 12, body, 0)
         part = 2 * y + h
-        for n in range(6):
+
+        def send(n):
             mine = is_own(chunk, n)
 
             @pl.when(mine)
@@ -222,6 +221,12 @@
             @pl.when(jnp.logical_not(mine))
             def _():
                 sigma_copy(chunk, n).start()
+
+        for n in range(6):
+            lax.fori_loop(0, 2, functools.partial(body, n), 0)
+            if n:
+                send(n - 1)
+        send(5)
 
     def out_ref(chunk, j):
         return (less_out, great_out)[chunk // 2].at[j, chunk % 2]

time: 83.3 us -> 82.2 us (0.987)
  the two profiles are of different devices: /device:TPU:100 before, /device:TPU:96 now
where the time goes in v2:
time: 82.2 us; the launch traced here: 82.1 us
  Pallas kernels  79 us (96%)
  local copies, waits for them, and re-layouts  2.44 us (3%)
    pallas_call x1, Pallas kernels, on_device(): pl.pallas_call(functools.partial(kernel, n_en), out_shape=(jax.ShapeDtype...  79 us
    unnamed x6, local copies, waits for them, and re-layouts  2.44 us

profile of v2, /device:TPU:96, one launch (start us, length us, event | category | flops | bytes accessed | tf_op | source)
XLA Modules:
  0.0 82.1 jit_solution(7166004431145526593)
XLA Ops:
  0.6 0.0 copy-start.1
  0.6 0.0 copy-start
  0.7 0.7 copy-done.1
  1.3 0.0 copy-done
  1.3 79.0 %born_update.1 = (bf16[3,2,128,512]{3,2,1,0:T(8,128)(2,1)S(1)}, bf16[3,2,128,512]{3,2,1,0:T(8,128)(2,1)S(1)}) custom-call(s32[2,3]{1,0:T(2,128)S(1)} %bitcast.2, f32[2,3]{1,0:T(2,128)S(1)} %bitcast.3, bf16[3,2,128,512]{3,2,1,0:T(8,128)(2,1)} %less_ref.1, bf16[3,2,128,512]{3,2,1,0:T(8,128)(2,1)} %great_ref.1, bf16[3,2,128,512]{3,2,1,0:T(8,128)(2,1)} %inv_ref.1), custom_call_target="tpu_custom_call" | custom-call | tf_op jit(solution)/shard_map/born_update/pallas_call | solution.py:322
  80.3 0.9 %copy.9 = bf16[3,2,128,512]{3,2,1,0:T(8,128)(2,1)} copy(bf16[3,2,128,512]{3,2,1,0:T(8,128)(2,1)S(1)} %get-tuple-element.4) | data formatting | bytes 1572864
  81.2 0.9 %copy.10 = bf16[3,2,128,512]{3,2,1,0:T(8,128)(2,1)} copy(bf16[3,2,128,512]{3,2,1,0:T(8,128)(2,1)S(1)} %get-tuple-element.5) | data formatting | bytes 1572864
Async XLA Ops:
  0.6 0.7 copy-start.1
  0.6 0.7 copy-start

commit v3 on v2

--- a/solution.py
+++ b/solution.py
@@ -250,17 +250,22 @@
             sigma = whole[chunk].reshape(512, 512)
             inverse = invs[slot].reshape(512, 512)
 
-            for r in range(2):
+            for r in (1 - y // 2, y // 2):
                 rows = invs[slot, pl.ds(2 * r, 2)].reshape(256, 512)
                 left = jnp.dot(rows, sigma, preferred_element_type=jnp.float32).astype(jnp.bfloat16)
                 result = lax.dot_general(
                     left, inverse, (((1,), (1,)), ((), ())), preferred_element_type=jnp.float32
                 )
                 prod[chunk, pl.ds(2 * r, 2)] = result.astype(jnp.bfloat16).reshape(2, 128, 512)
-            for d in (2, 1, 3):
-                out_copy(chunk, d).start()
-            j = energy_of(chunk)
-            pltpu.make_async_copy(prod.at[chunk, y], out_ref(chunk, j), out_recv.at[chunk, j]).start()
+                for d in (2, 1, 3, 0):
+
+                    @pl.when(lax.rem(y + d, 4) // 2 == r)
+                    def _():
+                        if d:
+                            out_copy(chunk, d).start()
+                        else:
+                            j = energy_of(chunk)
+                            pltpu.make_async_copy(prod.at[chunk, y], out_ref(chunk, j), out_recv.at[chunk, j]).start()
 
     def gather_inverses():
         for slot in range(2):

time: 82.2 us -> 82.7 us (level)
  the two profiles are of different devices: /device:TPU:96 before, /device:TPU:228 now
where the time goes in v3:
time: 82.7 us; the launch traced here: 82.6 us
  Pallas kernels  79.5 us (96%)
  local copies, waits for them, and re-layouts  2.44 us (3%)
    pallas_call x1, Pallas kernels, on_device(): pl.pallas_call(functools.partial(kernel, n_en), out_shape=(jax.ShapeDtype...  79.5 us
    unnamed x6, local copies, waits for them, and re-layouts  2.44 us

profile of v3, /device:TPU:228, one launch (start us, length us, event | category | flops | bytes accessed | tf_op | source)
XLA Modules:
  0.0 82.6 jit_solution(1454833766850344321)
XLA Ops:
  0.6 0.0 copy-start.1
  0.6 0.0 copy-start
  0.7 0.7 copy-done.1
  1.3 0.0 copy-done
  1.3 79.5 %born_update.1 = (bf16[3,2,128,512]{3,2,1,0:T(8,128)(2,1)S(1)}, bf16[3,2,128,512]{3,2,1,0:T(8,128)(2,1)S(1)}) custom-call(s32[2,3]{1,0:T(2,128)S(1)} %bitcast.2, f32[2,3]{1,0:T(2,128)S(1)} %bitcast.3, bf16[3,2,128,512]{3,2,1,0:T(8,128)(2,1)} %less_ref.1, bf16[3,2,128,512]{3,2,1,0:T(8,128)(2,1)} %great_ref.1, bf16[3,2,128,512]{3,2,1,0:T(8,128)(2,1)} %inv_ref.1), custom_call_target="tpu_custom_call" | custom-call | tf_op jit(solution)/shard_map/born_update/pallas_call | solution.py:327
  80.8 0.9 %copy.9 = bf16[3,2,128,512]{3,2,1,0:T(8,128)(2,1)} copy(bf16[3,2,128,512]{3,2,1,0:T(8,128)(2,1)S(1)} %get-tuple-element.4) | data formatting | bytes 1572864
  81.7 0.9 %copy.10 = bf16[3,2,128,512]{3,2,1,0:T(8,128)(2,1)} copy(bf16[3,2,128,512]{3,2,1,0:T(8,128)(2,1)S(1)} %get-tuple-element.5) | data formatting | bytes 1572864
Async XLA Ops:
  0.6 0.7 copy-start.1
  0.6 0.7 copy-start
